TPU v7x, 32 devices: a whole 2x2x4 slice. The times are simulated.
32 devices in a mesh: groups: 2 (over x), pts: 16 (over z, y, core).
Axes of the slice: x: 2, y: 2, z: 4, core: 2. Of those that a mesh axis runs over, the one named last changes fastest.
Arguments:
- points: bfloat16 [8192, 512], P(('groups', 'pts')), parts along dimension 0, may hold values from -6 to 6
- labels: int32 [8192], P(('groups', 'pts')), parts along dimension 0, may hold values from 0 to 15
- centres: bfloat16 [32768, 512], P(('groups', 'pts')), parts along dimension 0, may hold values from -6 to 6
- tri_inverse: bfloat16 [32768, 16384], P(('groups', 'pts')), parts along dimension 0, as said below
- beta: bfloat16 [32768, 16], P(('groups', 'pts')), parts along dimension 0, may hold values from -0.01171875 to 0.01171875
- bias: float32 [32], P('groups'), parts along dimension 0, may hold values from -3.2 to -2.2
Outputs:
- gradient: float32 [32768, 16], P(('groups', 'pts')), parts along dimension 0
- logits: float32 [8192, 16], P(('groups', 'pts')), parts along dimension 0
There are 2 independent parts, one for each index of `groups`. A program takes and returns all parts, laid end to end along the dimension named above; each array names one. Nothing has to cross between parts.
Inputs may be any that keep to these rules, and one draw needn't show every extreme that they name: `tri_inverse`: upper triangular: entries below the diagonal are zero; the diagonal lies between 0.6 and 1.4.
All inputs are finite; a program needn't handle non-finite values.
Results may differ from a plain program's by a relative error of at most 0.0039.
Values may be sent and summed in bfloat16 or wider, within the bound.
A program may use at most 128 MiB of HBM per device.

v0:
```python
import math

import jax
import jax.numpy as jnp
from jax import lax
from jax.sharding import PartitionSpec as P


def cube_kernel(point_block, centre_block):
    inner = lax.dot_general(
        point_block, centre_block, (((1,), (1,)), ((), ())), preferred_element_type=jnp.float32
    )
    factor = 1.0 / math.sqrt(point_block.shape[1])
    return ((inner * factor + 1.0) ** 3).astype(jnp.bfloat16)


def on_device(points, labels, centres, tri_inverse, beta, bias):
    local_points = points.shape[0]
    local_centres = centres.shape[0]
    class_count = beta.shape[1]
    packing = 128 // class_count
    dense_centres = local_centres // packing
    total_points = local_points * lax.axis_size("pts")
    beta_dense = beta.reshape(dense_centres, 128)
    beta_part = lax.all_gather(beta_dense, "pts", axis=0, tiled=True)
    narrow = beta_part.reshape(beta_part.shape[0] * packing, class_count)
    columns = tri_inverse
    alpha_sum = jnp.dot(columns, narrow, preferred_element_type=jnp.float32)
    alpha_local = alpha_sum.astype(jnp.bfloat16)
    alpha_dense = alpha_local.reshape(dense_centres, 128)
    classes_row = jnp.arange(class_count, dtype=jnp.int32)
    onehot = (labels[:, None] == classes_row[None, :]).astype(jnp.float32)
    parts_in = (
        lax.all_gather(centres, "pts", axis=0, tiled=True),
        lax.all_gather(alpha_dense, "pts", axis=0, tiled=True),
    )
    kernel_tile = cube_kernel(points, parts_in[0])
    narrow = parts_in[1].reshape(parts_in[1].shape[0] * packing, class_count)
    logit_sum = jnp.dot(kernel_tile, narrow, preferred_element_type=jnp.float32)
    logits = logit_sum + bias[None, :]
    resid = (jax.nn.sigmoid(logits) - onehot).astype(jnp.bfloat16)
    resid_dense = resid.reshape(local_points // packing, 128)
    parts_in = (
        lax.all_gather(points, "pts", axis=0, tiled=True),
        lax.all_gather(resid_dense, "pts", axis=0, tiled=True),
    )
    kernel_tile = cube_kernel(parts_in[0], centres)
    narrow = parts_in[1].reshape(parts_in[1].shape[0] * packing, class_count)
    grad_sum = lax.dot_general(
        kernel_tile, narrow, (((0,), (0,)), ((), ())), preferred_element_type=jnp.float32
    )
    grad_dense = grad_sum.reshape(dense_centres, 128)
    grad_kernel = (
        grad_dense.reshape(local_centres, class_count) * (1.0 / math.sqrt(total_points))
    ).astype(jnp.bfloat16)
    columns = tri_inverse
    term = lax.dot_general(
        columns, grad_kernel, (((0,), (0,)), ((), ())), preferred_element_type=jnp.float32
    )
    gradient_dense = lax.psum_scatter(
        term.reshape(lax.axis_size("pts") * dense_centres, 128),
        "pts",
        scatter_dimension=0,
        tiled=True,
    )
    return (gradient_dense.reshape(local_centres, class_count), logits)


def solution(mesh):
    return jax.shard_map(
        on_device,
        mesh=mesh,
        in_specs=(
            P(("groups", "pts"), None),
            P(("groups", "pts")),
            P(("groups", "pts"), None),
            P(("groups", "pts"), None),
            P(("groups", "pts"), None),
            P("groups"),
        ),
        out_specs=(P(("groups", "pts"), None), P(("groups", "pts"), None)),
        check_vma=False,
    )
```

profile of v0, /device:TPU:16, one launch (start us, length us, event | category | flops | bytes accessed | tf_op | source)
XLA Modules:
  0.0 292.6 jit_solution(16298011855423108095)
XLA Ops:
  7.2 0.0 all-gather.5.cloned.1.call-start
  7.2 0.7 all-gather.5.cloned.1.call-update
  7.9 0.0 all-gather.3.cloned.1.call-start
  7.9 0.7 all-gather.3.cloned.1.call-update
  8.6 0.0 reduce-scatter.2.cloned.1.call-start
  8.7 0.9 copy.8
  9.6 0.2 reshape.30
  9.8 19.6 %all_gather.17 = bf16[2048,128]{1,0:T(8,128)(2,1)S(1)} all-gather(bf16[128,128]{1,0:T(8,128)(2,1)S(1)} %reshape.30), channel_id=1, replica_groups=mesh['groups'=2,'pts'=16] {'pts'}, dimensions={0}, use_global_device_ids=true | all-gather | bytes 557056 | tf_op jit(solution)/shard_map/all_gather | solution.py:25
  29.4 4.0 %reshape.31 = bf16[16384,16]{1,0:T(8,128)(2,1)} reshape(bf16[2048,128]{1,0:T(8,128)(2,1)S(1)} %all_gather.17) | data formatting | bytes 1048576 | tf_op jit(solution)/shard_map/reshape | solution.py:26
  33.4 15.4 %convolution_convert_fusion = bf16[1024,16]{0,1:T(8,128)(2,1)S(1)} fusion(bf16[1024,16384]{1,0:T(8,128)(2,1)} %param.9, bf16[16384,16]{1,0:T(8,128)(2,1)} %reshape.31), kind=kOutput, calls=%fused_computation.11 | convolution fusion | flops 536887296 | bytes 34111488 | tf_op jit(solution)/shard_map/dot_general | solution.py:28
  48.8 0.2 copy.9
  49.0 0.2 reshape.32
  49.2 21.6 %all_gather.18 = bf16[2048,128]{1,0:T(8,128)(2,1)S(1)} all-gather(bf16[128,128]{1,0:T(8,128)(2,1)S(1)} %reshape.32), channel_id=1, replica_groups=mesh['groups'=2,'pts'=16] {'pts'}, dimensions={0}, use_global_device_ids=true | all-gather | bytes 557056 | tf_op jit(solution)/shard_map/all_gather | solution.py:35
  70.8 4.0 %reshape.33 = bf16[16384,16]{1,0:T(8,128)(2,1)} reshape(bf16[2048,128]{1,0:T(8,128)(2,1)S(1)} %all_gather.18) | data formatting | bytes 1048576 | tf_op jit(solution)/shard_map/reshape | solution.py:38
  74.8 64.8 %all-gather.5.cloned.1.call-done = bf16[16384,512]{1,0:T(8,128)(2,1)} async-done(((bf16[1024,512]{1,0:T(8,128)(2,1)}), bf16[16384,512]{1,0:T(8,128)(2,1)}) %all-gather.5.cloned.1.call-update) | async-done | bytes 16777232 | tf_op jit(solution)/shard_map/all_gather | solution.py:34
  139.7 0.0 copy-done.1
  139.7 0.0 copy-done.2
  139.7 0.0 copy-done.3
  139.7 11.7 %subtract_convert_fusion = (bf16[256,16]{0,1:T(8,128)(2,1)S(1)}, f32[256,16]{0,1:T(8,128)}) fusion(s32[256]{0:T(256)S(1)} %copy-done.2, f32[16]{0:T(128)S(1)} %copy-done.3, bf16[16384,16]{1,0:T(8,128)(2,1)} %reshape.33, bf16[256,512]{1,0:T(8,128)(2,1)S(1)} %copy-done.1, bf16[16384,512]{1,0:T(8,128)(2,1)} %all-gather.5.cloned.1.call-done), kind=kOutput, calls=%fused_computation.13 | convolution fusion | flops 4450189312 | bytes 17589312 | tf_op jit(solution)/shard_map/dot_general | solution.py:39
  151.4 0.1 copy.10
  151.5 0.1 reshape.34
  151.6 14.6 %all_gather.19 = bf16[512,128]{1,0:T(8,128)(2,1)S(1)} all-gather(bf16[32,128]{1,0:T(8,128)(2,1)S(1)} %reshape.34), channel_id=1, replica_groups=mesh['groups'=2,'pts'=16] {'pts'}, dimensions={0}, use_global_device_ids=true | all-gather | bytes 139264 | tf_op jit(solution)/shard_map/all_gather | solution.py:45
  166.2 0.7 reshape.35
  166.9 24.4 %all-gather.3.cloned.1.call-done = bf16[4096,512]{1,0:T(8,128)(2,1)} async-done(((bf16[256,512]{1,0:T(8,128)(2,1)}), bf16[4096,512]{1,0:T(8,128)(2,1)}) %all-gather.3.cloned.1.call-update) | async-done | bytes 4194320 | tf_op jit(solution)/shard_map/all_gather | solution.py:44
  191.2 12.9 %fusion.10 = bf16[1024,16]{1,0:T(8,128)(2,1)S(1)} fusion(bf16[4096,16]{1,0:T(8,128)(2,1)S(1)} %reshape.35, bf16[4096,512]{1,0:T(8,128)(2,1)} %all-gather.3.cloned.1.call-done, bf16[1024,512]{1,0:T(8,128)(2,1)S(1)} %copy-done), kind=kOutput, calls=%fused_computation.10 | convolution fusion | flops 4450189312 | bytes 5406720 | tf_op jit(solution)/shard_map/dot_general | solution.py:49
  204.1 13.1 %convolution_bitcast_fusion = f32[16384,16]{0,1:T(8,128)S(1)} fusion(bf16[1024,16]{1,0:T(8,128)(2,1)S(1)} %fusion.10, bf16[1024,16384]{1,0:T(8,128)(2,1)} %param.9), kind=kOutput, calls=%fused_computation.5 | convolution fusion | flops 536870912 | bytes 34635776 | tf_op jit(solution)/shard_map/dot_general | solution.py:57
  217.2 4.6 %copy.11 = f32[16384,16]{1,0:T(8,128)} copy(f32[16384,16]{0,1:T(8,128)S(1)} %convolution_bitcast_fusion) | data formatting | bytes 2097152 | tf_op jit(solution)/shard_map/dot_general | solution.py:57
  221.8 6.5 %reshape.36 = f32[2048,128]{1,0:T(8,128)} reshape(f32[16384,16]{1,0:T(8,128)} %copy.11) | data formatting | bytes 2097152 | tf_op jit(solution)/shard_map/reshape | solution.py:61
  228.3 0.0 reduce-scatter.2.cloned.1.call-update
  228.3 55.9 %reduce-scatter.2.cloned.1.call-done = f32[128,128]{1,0:T(8,128)} async-done(((f32[2048,128]{1,0:T(8,128)}), f32[128,128]{1,0:T(8,128)}) %reduce-scatter.2.cloned.1.call-update) | async-done | bytes 65552 | tf_op jit(solution)/shard_map/reduce_scatter | solution.py:60
  284.2 1.0 reshape.37
  285.2 0.8 copy.12
  (5 shorter events, 0.0 us)
Async XLA Ops:
  7.2 132.5 %all-gather.5.cloned.1.call-start = ((), (), s32[]{:S(2)}) async-start(), calls=%async_computation.2 | async-start | bytes 17825792 | tf_op jit(solution)/shard_map/all_gather | solution.py:34
  7.9 183.3 %all-gather.3.cloned.1.call-start = ((), (), s32[]{:S(2)}) async-start(), calls=%async_computation.1 | async-start | bytes 4456448 | tf_op jit(solution)/shard_map/all_gather | solution.py:44
  8.6 275.6 %reduce-scatter.2.cloned.1.call-start = ((), (), s32[]{:S(2)}) async-start(), calls=%async_computation.3 | async-start | bytes 1114112 | tf_op jit(solution)/shard_map/reduce_scatter | solution.py:60
  33.4 106.3 %copy-start.1 = (bf16[256,512]{1,0:T(8,128)(2,1)S(1)}, bf16[256,512]{1,0:T(8,128)(2,1)}, u32[]{:S(2)}) copy-start(bf16[256,512]{1,0:T(8,128)(2,1)} %param.6) | copy-start | bytes 786436
  33.4 106.3 %copy-start.2 = (s32[256]{0:T(256)S(1)}, s32[256]{0:T(256)}, u32[]{:S(2)}) copy-start(s32[256]{0:T(256)} %param.7) | copy-start | bytes 3076
  33.4 106.3 %copy-start.3 = (f32[16]{0:T(128)S(1)}, f32[16]{0:T(128)}, u32[]{:S(2)}) copy-start(f32[16]{0:T(128)} %param.11) | copy-start | bytes 196
  74.8 116.4 %copy-start = (bf16[1024,512]{1,0:T(8,128)(2,1)S(1)}, bf16[1024,512]{1,0:T(8,128)(2,1)}, u32[]{:S(2)}) copy-start(bf16[1024,512]{1,0:T(8,128)(2,1)} %param.8) | copy-start | bytes 3145732
Sparse Core Ops, SparseCore 0:
  10.1 129.5 all-gather.4
  141.9 49.3 all-gather.2
  228.4 55.7 reduce-scatter.1
where the time goes:
time: 296 us; the launch traced here: 293 us
  waiting for transfers between devices  147 us (50%)
  blocking collectives  55.8 us (19%)
  matrix products  53.1 us (18%)
  local copies, waits for them, and re-layouts  23.3 us (8%)
  between operations  13.8 us (5%)
    all_gather x1, waiting for transfers between devices, on_device(): lax.all_gather(centres, 'pts', axis=0, tiled=True)  64.8 us
    reduce_scatter x1, waiting for transfers between devices, on_device(): lax.psum_scatter(term.reshape(lax.axis_size('pts') * dense_centres, 128),...  55.9 us
    all_gather x1, waiting for transfers between devices, on_device(): lax.all_gather(points, 'pts', axis=0, tiled=True)  24.4 us
    all_gather x1, blocking collectives, on_device(): lax.all_gather(alpha_dense, 'pts', axis=0, tiled=True)  21.6 us
    all_gather x1, blocking collectives, on_device(): beta_part = lax.all_gather(beta_dense, 'pts', axis=0, tiled=True)  19.6 us
    dot_general x1, matrix products, on_device(): alpha_sum = jnp.dot(columns, narrow, preferred_element_type=jnp.float32)  15.4 us
    all_gather x1, blocking collectives, on_device(): lax.all_gather(resid_dense, 'pts', axis=0, tiled=True)  14.6 us
    dot_general x1, matrix products, on_device(): lax.dot_general(columns, grad_kernel, (((0,), (0,)), ((), ())), preferred...  13.1 us
  transfers between devices with their start and end apart: 3, of which 3 were waited for; matrix products, arithmetic and copies ran while one was open for 13% of the time, Pallas kernels for 0%

commit v1 on v0

--- a/solution.py
+++ b/solution.py
@@ -27,25 +27,19 @@
     columns = tri_inverse
     alpha_sum = jnp.dot(columns, narrow, preferred_element_type=jnp.float32)
     alpha_local = alpha_sum.astype(jnp.bfloat16)
-    alpha_dense = alpha_local.reshape(dense_centres, 128)
     classes_row = jnp.arange(class_count, dtype=jnp.int32)
     onehot = (labels[:, None] == classes_row[None, :]).astype(jnp.float32)
-    parts_in = (
-        lax.all_gather(centres, "pts", axis=0, tiled=True),
-        lax.all_gather(alpha_dense, "pts", axis=0, tiled=True),
+    points_all = lax.all_gather(points, "pts", axis=0, tiled=True)
+    kernel_tile = cube_kernel(points_all, centres)
+    logit_part = jnp.dot(kernel_tile, alpha_local, preferred_element_type=jnp.float32)
+    logit_dense = lax.psum_scatter(
+        logit_part.reshape(total_points // packing, 128), "pts", scatter_dimension=0, tiled=True
     )
-    kernel_tile = cube_kernel(points, parts_in[0])
-    narrow = parts_in[1].reshape(parts_in[1].shape[0] * packing, class_count)
-    logit_sum = jnp.dot(kernel_tile, narrow, preferred_element_type=jnp.float32)
-    logits = logit_sum + bias[None, :]
+    logits = logit_dense.reshape(local_points, class_count) + bias[None, :]
     resid = (jax.nn.sigmoid(logits) - onehot).astype(jnp.bfloat16)
     resid_dense = resid.reshape(local_points // packing, 128)
-    parts_in = (
-        lax.all_gather(points, "pts", axis=0, tiled=True),
-        lax.all_gather(resid_dense, "pts", axis=0, tiled=True),
-    )
-    kernel_tile = cube_kernel(parts_in[0], centres)
-    narrow = parts_in[1].reshape(parts_in[1].shape[0] * packing, class_count)
+    resid_all = lax.all_gather(resid_dense, "pts", axis=0, tiled=True)
+    narrow = resid_all.reshape(total_points, class_count)
     grad_sum = lax.dot_general(
         kernel_tile, narrow, (((0,), (0,)), ((), ())), preferred_element_type=jnp.float32
     )

time: 296 us -> 269 us (0.909)
  blocking collectives: 55.8 us -> 35.1 us
  waiting for transfers between devices: 147 us -> 142 us
    all_gather x2 -> x1, waiting for transfers between devices: 89.2 us -> 30.5 us  [on_device(): points_all = lax.all_gather(points, 'pts', axis=0, tiled=True)]
    reduce_scatter x0 -> x1, waiting for transfers between devices: none -> 53.5 us  [on_device(): lax.psum_scatter(logit_part.reshape(total_points // packing, 128), 'pts',...]
    all_gather x2 -> x1, blocking collectives: 36.2 us -> 16.4 us  [on_device(): resid_all = lax.all_gather(resid_dense, 'pts', axis=0, tiled=True)]
    dot_general x3 -> x2, matrix products: 40 us -> 33.6 us  [the longest x1 23.9 us: on_device(): jnp.dot(kernel_tile, alpha_local, preferred_element_type=jnp.float32)]
    dot_general x1, matrix products: 13.1 us -> 18.7 us  [on_device(): lax.dot_general(columns, grad_kernel, (((0,), (0,)), ((), ())), preferred...]
  transfers between devices with their start and end apart: 3 -> 3, of which waited for: 3 -> 3; matrix products, arithmetic and copies ran while one was open for 13% -> 2% of each run, Pallas kernels for 0% -> 0%
where the time goes in v1:
time: 269 us; the launch traced here: 266 us
  waiting for transfers between devices  142 us (53%)
  matrix products  52.2 us (19%)
  blocking collectives  35.1 us (13%)
  local copies, waits for them, and re-layouts  21.2 us (8%)
  between operations  13.8 us (5%)
    reduce_scatter x1, waiting for transfers between devices, on_device(): lax.psum_scatter(term.reshape(lax.axis_size('pts') * dense_centres, 128),...  57.7 us
    reduce_scatter x1, waiting for transfers between devices, on_device(): lax.psum_scatter(logit_part.reshape(total_points // packing, 128), 'pts',...  53.5 us
    all_gather x1, waiting for transfers between devices, on_device(): points_all = lax.all_gather(points, 'pts', axis=0, tiled=True)  30.5 us
    dot_general x1, matrix products, on_device(): jnp.dot(kernel_tile, alpha_local, preferred_element_type=jnp.float32)  23.9 us
    all_gather x1, blocking collectives, on_device(): beta_part = lax.all_gather(beta_dense, 'pts', axis=0, tiled=True)  18.7 us
    dot_general x1, matrix products, on_device(): lax.dot_general(columns, grad_kernel, (((0,), (0,)), ((), ())), preferred...  18.7 us
    all_gather x1, blocking collectives, on_device(): resid_all = lax.all_gather(resid_dense, 'pts', axis=0, tiled=True)  16.4 us
    dot_general x1, matrix products, cube_kernel(): lax.dot_general(point_block, centre_block, (((1,), (1,)), ((), ())), pref...  9.7 us
  transfers between devices with their start and end apart: 3, of which 3 were waited for; matrix products, arithmetic and copies ran while one was open for 2% of the time, Pallas kernels for 0%

profile of v1, /device:TPU:16, one launch (start us, length us, event | category | flops | bytes accessed | tf_op | source)
XLA Modules:
  0.0 265.6 jit_solution(8832059732603507491)
XLA Ops:
  7.2 0.0 all-gather.2.cloned.1.call-start
  7.2 0.7 all-gather.2.cloned.1.call-update
  7.9 0.0 reduce-scatter.3.cloned.1.call-start
  8.0 0.9 copy.8
  8.9 0.2 reshape.33
  9.1 18.7 %all_gather.10 = bf16[2048,128]{1,0:T(8,128)(2,1)S(1)} all-gather(bf16[128,128]{1,0:T(8,128)(2,1)S(1)} %reshape.33), channel_id=1, replica_groups=mesh['groups'=2,'pts'=16] {'pts'}, dimensions={0}, use_global_device_ids=true | all-gather | bytes 557056 | tf_op jit(solution)/shard_map/all_gather | solution.py:25
  27.8 4.0 %reshape.34 = bf16[16384,16]{1,0:T(8,128)(2,1)} reshape(bf16[2048,128]{1,0:T(8,128)(2,1)S(1)} %all_gather.10) | data formatting | bytes 1048576 | tf_op jit(solution)/shard_map/reshape | solution.py:26
  31.8 30.5 %all-gather.2.cloned.1.call-done = bf16[4096,512]{1,0:T(8,128)(2,1)} async-done(((bf16[256,512]{1,0:T(8,128)(2,1)}), bf16[4096,512]{1,0:T(8,128)(2,1)}) %all-gather.2.cloned.1.call-update) | async-done | bytes 4194320 | tf_op jit(solution)/shard_map/all_gather | solution.py:32
  62.2 9.7 %fusion = bf16[4096,1024]{1,0:T(8,128)(2,1)} fusion(bf16[4096,512]{1,0:T(8,128)(2,1)} %all-gather.2.cloned.1.call-done, bf16[1024,512]{1,0:T(8,128)(2,1)S(1)} %copy-done), kind=kOutput, calls=%fused_computation.2 | convolution fusion | flops 4315938816 | bytes 13631488 | tf_op jit(solution)/shard_map/dot_general | solution.py:10
  71.9 23.9 %fusion.2 = f32[4096,16]{1,0:T(8,128)S(1)} fusion(bf16[4096,1024]{1,0:T(8,128)(2,1)} %fusion, bf16[1024,16384]{1,0:T(8,128)(2,1)} %param.9, bf16[16384,16]{1,0:T(8,128)(2,1)} %reshape.34), kind=kOutput, calls=%fused_computation.6 | convolution fusion | flops 671105024 | bytes 42729472 | tf_op jit(solution)/shard_map/dot_general | solution.py:34
  95.8 1.3 reshape.35
  97.1 0.0 reduce-scatter.3.cloned.1.call-update
  97.1 0.0 reduce-scatter.5.cloned.1.call-start
  97.2 0.1 eq.22
  97.3 0.1 copy.10
  97.4 0.1 copy.11
  97.4 0.1 add.34
  97.5 0.1 eq.26
  97.6 53.5 %reduce-scatter.3.cloned.1.call-done = f32[32,128]{1,0:T(8,128)} async-done(((f32[512,128]{1,0:T(8,128)}), f32[32,128]{1,0:T(8,128)}) %reduce-scatter.3.cloned.1.call-update) | async-done | bytes 16400 | tf_op jit(solution)/shard_map/reduce_scatter | solution.py:35
  151.1 0.7 subtract_convert_fusion
  151.9 16.4 %all_gather.11 = bf16[512,128]{1,0:T(8,128)(2,1)S(1)} all-gather(bf16[32,128]{1,0:T(8,128)(2,1)S(1)} %subtract_convert_fusion), channel_id=1, replica_groups=mesh['groups'=2,'pts'=16] {'pts'}, dimensions={0}, use_global_device_ids=true | all-gather | bytes 139264 | tf_op jit(solution)/shard_map/all_gather | solution.py:41
  168.2 0.7 reshape.36
  168.9 18.7 %convolution_bitcast_fusion = f32[16384,16]{0,1:T(8,128)S(1)} fusion(bf16[1024,16384]{1,0:T(8,128)(2,1)} %param.9, bf16[4096,1024]{1,0:T(8,128)(2,1)} %fusion, bf16[4096,16]{1,0:T(8,128)(2,1)S(1)} %reshape.36), kind=kOutput, calls=%fused_computation.1 | convolution fusion | flops 671121408 | bytes 43122688 | tf_op jit(solution)/shard_map/dot_general | solution.py:51
  187.6 0.0 copy-start.1
  187.6 4.6 %copy.12 = f32[16384,16]{1,0:T(8,128)} copy(f32[16384,16]{0,1:T(8,128)S(1)} %convolution_bitcast_fusion) | data formatting | bytes 2097152 | tf_op jit(solution)/shard_map/dot_general | solution.py:51
  192.2 6.5 %reshape.37 = f32[2048,128]{1,0:T(8,128)} reshape(f32[16384,16]{1,0:T(8,128)} %copy.12) | data formatting | bytes 2097152 | tf_op jit(solution)/shard_map/reshape | solution.py:55
  198.7 0.0 reduce-scatter.5.cloned.1.call-update
  198.7 0.1 reshape.39
  198.8 0.7 copy.14
  199.5 57.7 %reduce-scatter.5.cloned.1.call-done = f32[128,128]{1,0:T(8,128)} async-done(((f32[2048,128]{1,0:T(8,128)}), f32[128,128]{1,0:T(8,128)}) %reduce-scatter.5.cloned.1.call-update) | async-done | bytes 65552 | tf_op jit(solution)/shard_map/reduce_scatter | solution.py:54
  257.2 1.0 reshape.38
  258.3 0.8 copy.13
  (13 shorter events, 0.1 us)
Async XLA Ops:
  7.2 55.1 %copy-start = (bf16[1024,512]{1,0:T(8,128)(2,1)S(1)}, bf16[1024,512]{1,0:T(8,128)(2,1)}, u32[]{:S(2)}) copy-start(bf16[1024,512]{1,0:T(8,128)(2,1)} %param.8) | copy-start | bytes 3145732
  7.2 55.1 %all-gather.2.cloned.1.call-start = ((), (), s32[]{:S(2)}) async-start(), calls=%async_computation.2 | async-start | bytes 4456448 | tf_op jit(solution)/shard_map/all_gather | solution.py:32
  7.9 143.2 %reduce-scatter.3.cloned.1.call-start = ((), (), s32[]{:S(2)}) async-start(), calls=%async_computation.3 | async-start | bytes 278528 | tf_op jit(solution)/shard_map/reduce_scatter | solution.py:35
  71.9 25.2 %copy-start.4 = (s32[256]{0:T(256)S(1)}, s32[256]{0:T(256)}, u32[]{:S(2)}) copy-start(s32[256]{0:T(256)} %param.7) | copy-start | bytes 3076
  71.9 25.5 %copy-start.3 = (f32[16]{0:T(128)S(1)}, f32[16]{0:T(128)}, u32[]{:S(2)}) copy-start(f32[16]{0:T(128)} %param.11) | copy-start | bytes 196
  97.1 160.1 %reduce-scatter.5.cloned.1.call-start = ((), (), s32[]{:S(2)}) async-start(), calls=%async_computation.4 | async-start | bytes 1114112 | tf_op jit(solution)/shard_map/reduce_scatter | solution.py:54
  187.6 11.1 %copy-start.2 = (f32[32,128]{1,0:T(8,128)S(1)}, f32[32,128]{1,0:T(8,128)}, u32[]{:S(2)}) copy-start(f32[32,128]{1,0:T(8,128)} %reduce-scatter.3.cloned.1.call-done) | copy-start | bytes 49156
  187.6 71.5 %copy-start.1 = (bf16[1024,512]{1,0:T(8,128)(2,1)S(1)}, bf16[1024,512]{1,0:T(8,128)(2,1)}, u32[]{:S(2)}) copy-start(bf16[1024,512]{1,0:T(8,128)(2,1)} %param.8) | copy-start | bytes 3145732
Sparse Core Ops, SparseCore 0:
  10.1 52.0 all-gather.1
  97.3 53.8 reduce-scatter.2
  198.8 58.3 reduce-scatter.4

commit v2 on v1

v2 whole, which is shorter than its diff:
```python
import functools
import math

import jax
import jax.numpy as jnp
from jax import lax
from jax.experimental import pallas as pl
from jax.experimental.pallas import tpu as pltpu
from jax.sharding import PartitionSpec as P

NT = (((1,), (1,)), ((), ()))
NN = (((1,), (0,)), ((), ()))


def dot(left, right, dims):
    return lax.dot_general(left, right, dims, preferred_element_type=jnp.float32)


def body(
    n, points, labels, centres, tri, beta, bias, grad_out, logits_out,
    tbuf, pbuf, cbuf, kbuf, bbuf, abuf, asum, lsend, lrecv, rbuf, gsend, grecv, tsend, trecv, total,
    t_sem, own_sem, b_send, b_recv, f_send, p_send, p_recv, c_send, c_recv, a_send, a_recv,
    l_send, l_recv, r_send, r_recv, g_send, g_recv, ts_sem, tr_sem,
):
    chips = n // 2
    depth = chips // 2
    me = lax.axis_index("pts")
    core = lax.rem(me, 2)
    chip = me // 2
    side = lax.rem(chip, 2)
    level = chip // 2
    partner = me + 1 - 2 * core
    size = centres.shape[0]
    factor = 1.0 / math.sqrt(points.shape[1])
    total_points = n * points.shape[0]
    classes = beta.shape[0]

    def remote(src, dst, send, recv, target):
        return pltpu.make_async_remote_copy(
            src_ref=src, dst_ref=dst, send_sem=send, recv_sem=recv,
            device_id={"pts": target}, device_id_type=pl.DeviceIdType.MESH,
        )

    def tri_copy(j):
        start = pl.multiple_of(j * size, size)
        return pltpu.make_async_copy(tri.at[:, pl.ds(start, size)], tbuf.at[j], t_sem.at[j])

    def each(count, fn):
        lax.fori_loop(0, count, lambda i, c: (fn(i), c)[1], 0)

    own_points = pltpu.make_async_copy(points, pbuf.at[chip], own_sem.at[0])
    own_centres = pltpu.make_async_copy(centres, cbuf.at[core], own_sem.at[1])
    own_points.start()
    own_centres.start()

    @functools.partial(each, n)
    def _(j):
        @pl.when(j >= me)
        def _():
            tri_copy(j).start()

    barrier = pltpu.get_barrier_semaphore()

    @functools.partial(each, n)
    def _(q):
        @pl.when(q != me)
        def _():
            pl.semaphore_signal(
                barrier, inc=1, device_id={"pts": q}, device_id_type=pl.DeviceIdType.MESH
            )

    pl.semaphore_wait(barrier, n - 1)

    def beta_send(q):
        return remote(beta, bbuf.at[me], b_send.at[q], b_recv.at[me], 2 * q + core)

    def beta_pass(q):
        block = 2 * q + core
        return remote(bbuf.at[block], bbuf.at[block], f_send.at[q], b_recv.at[block], partner)

    own_pass = remote(beta, bbuf.at[me], f_send.at[chip], b_recv.at[me], partner)
    centre_pass = remote(centres, cbuf.at[core], c_send, c_recv, partner)

    @functools.partial(each, chips)
    def _(q):
        @pl.when(q != chip)
        def _():
            beta_send(q).start()

    own_pass.start()
    centre_pass.start()
    bbuf[me] = beta[...]

    def chip_of(lev, sid):
        return 2 * lev + sid

    def point_copy(way, block):
        target = (chip + 2, chip - 2, chip_of(level, 1 - side))[way]
        return remote(
            pbuf.at[block], pbuf.at[block], p_send.at[way, block], p_recv.at[block],
            2 * target + core,
        )

    def point_sends(lev, act):
        block = chip_of(lev, side)
        for way, wanted in (
            (2, True),
            (0, (lev <= level) & (level < depth - 1)),
            (1, (lev >= level) & (level > 0)),
        ):
            @pl.when(wanted)
            def _():
                act(point_copy(way, block))

    own_points.wait()
    point_sends(level, lambda c: c.start())

    @functools.partial(each, chips)
    def _(q):
        @pl.when(q != chip)
        def _():
            remote(
                beta, bbuf.at[2 * q + core], b_send.at[q], b_recv.at[2 * q + core], partner
            ).wait_recv()
            beta_pass(q).start()

    own_centres.wait()
    remote(centres, cbuf.at[1 - core], c_send, c_recv, partner).wait_recv()

    def make_tile(block):
        for half in range(2):
            inner = dot(pbuf[block], cbuf[half], NT)
            value = inner * factor + 1.0
            kbuf[block, half] = (value * value * value).astype(jnp.bfloat16)

    make_tile(chip)

    @functools.partial(each, chips)
    def _(q):
        block = 2 * q + 1 - core
        remote(beta, bbuf.at[block], b_send.at[q], b_recv.at[block], partner).wait_recv()

    asum[...] = jnp.zeros_like(asum)

    def add_alpha(j):
        @pl.when((j >= me) & (j < n))
        def _():
            tri_copy(j).wait()
            asum[...] += dot(bbuf[j], tbuf[j], NT)

    def point_wait(block):
        remote(
            pbuf.at[block], pbuf.at[block], p_send.at[0, block], p_recv.at[block], partner
        ).wait_recv()

    share = -(-n // max(depth - 1, 1))

    def logit_copy(block):
        return remote(
            lsend.at[block], lrecv.at[chip], l_send.at[block], l_recv.at[chip], 2 * block + core
        )

    def logit_part(block):
        part = dot(abuf[0], kbuf[block, 0], NT) + dot(abuf[1], kbuf[block, 1], NT)

        @pl.when(block != chip)
        def _():
            lsend[block] = part
            logit_copy(block).start()

        @pl.when(block == chip)
        def _():
            lrecv[block] = part

    alpha_pass = remote(abuf.at[core], abuf.at[core], a_send, a_recv, partner)

    def step(d):
        for sign in (-1, 1):
            lev = level + sign * d

            @pl.when((lev >= 0) & (lev < depth))
            def _():
                point_wait(chip_of(lev, side))
                point_sends(lev, lambda c: c.start())

        each(share, lambda i: add_alpha((d - 1) * share + i))

        for sign in (-1, 1):
            lev = level + sign * d

            @pl.when((lev >= 0) & (lev < depth))
            def _():
                make_tile(chip_of(lev, side))

        def across(lev):
            @pl.when((lev >= 0) & (lev < depth))
            def _():
                point_wait(chip_of(lev, 1 - side))
                make_tile(chip_of(lev, 1 - side))

        across(level - d + 1)

        @pl.when(d > 1)
        def _():
            across(level + d - 1)

    each(depth - 1, lambda i: step(i + 1))
    abuf[core] = asum[...].astype(jnp.bfloat16)
    alpha_pass.start()
    remote(abuf.at[core], abuf.at[1 - core], a_send, a_recv, partner).wait_recv()

    def is_late(block):
        lev = block // 2
        far = (lev - level == depth - 1) | (level - lev == depth - 1)
        return far & (lax.rem(block, 2) != side)

    @functools.partial(each, chips)
    def _(block):
        @pl.when(jnp.logical_not(is_late(block)))
        def _():
            logit_part(block)

    @functools.partial(each, chips)
    def _(block):
        @pl.when(is_late(block))
        def _():
            point_wait(block)
            make_tile(block)
            logit_part(block)

    @functools.partial(each, chips)
    def _(q):
        @pl.when(q != chip)
        def _():
            remote(lsend.at[q], lrecv.at[q], l_send.at[q], l_recv.at[q], partner).wait_recv()

    logits = lrecv[0]
    for q in range(1, chips):
        logits = logits + lrecv[q]
    logits = logits + bias[...]
    logits_out[...] = logits
    onehot = (labels[...] == lax.broadcasted_iota(jnp.int32, logits.shape, 0)).astype(jnp.float32)
    rbuf[chip] = (jax.nn.sigmoid(logits) - onehot).astype(jnp.bfloat16)

    def resid_copy(q):
        return remote(rbuf.at[chip], rbuf.at[chip], r_send.at[q], r_recv.at[chip], 2 * q + core)

    @functools.partial(each, chips)
    def _(q):
        @pl.when(q != chip)
        def _():
            resid_copy(q).start()

    @functools.partial(each, chips)
    def _(q):
        @pl.when(q != chip)
        def _():
            remote(rbuf.at[q], rbuf.at[q], r_send.at[q], r_recv.at[q], partner).wait_recv()

    def grad_half(half):
        return lax.fori_loop(
            0, chips, lambda q, acc: acc + dot(rbuf[q], kbuf[q, half], NN),
            jnp.zeros((classes, size), jnp.float32),
        )

    gsend[...] = grad_half(1 - core)
    grad_pass = remote(gsend, grecv, g_send, g_recv, partner)
    grad_pass.start()
    mine = grad_half(core)
    grad_pass.wait_recv()
    coeff = ((mine + grecv[...]) * (1.0 / math.sqrt(total_points))).astype(jnp.bfloat16)

    def term_copy(j):
        return remote(tsend.at[j], trecv.at[me], ts_sem.at[j], tr_sem.at[me], j)

    @functools.partial(each, n)
    def _(i):
        j = n - 1 - i

        @pl.when(j >= me)
        def _():
            term = dot(coeff, tbuf[j], NN)

            @pl.when(j == me)
            def _():
                total[...] = term

            @pl.when(j != me)
            def _():
                tsend[j] = term.astype(tsend.dtype)
                term_copy(j).start()

    @functools.partial(each, n)
    def _(q):
        @pl.when(q < me)
        def _():
            remote(tsend.at[q], trecv.at[q], ts_sem.at[q], tr_sem.at[q], partner).wait_recv()
            total[...] += trecv[q].astype(jnp.float32)

    grad_out[...] = total[...]

    @functools.partial(each, chips)
    def _(q):
        @pl.when(q != chip)
        def _():
            beta_send(q).wait_send()
            beta_pass(q).wait_send()
            logit_copy(q).wait_send()
            resid_copy(q).wait_send()

    own_pass.wait_send()
    centre_pass.wait_send()
    alpha_pass.wait_send()
    grad_pass.wait_send()
    each(depth, lambda lev: point_sends(lev, lambda c: c.wait_send()))

    @functools.partial(each, n)
    def _(j):
        @pl.when(j > me)
        def _():
            term_copy(j).wait_send()


def on_device(points, labels, centres, tri_inverse, beta, bias):
    n = lax.axis_size("pts")
    chips = n // 2
    rows, features = points.shape
    size, classes = beta.shape
    low, full = jnp.bfloat16, jnp.float32
    dma = pltpu.SemaphoreType.DMA
    vmem = pl.BlockSpec(memory_space=pltpu.VMEM)
    hbm = pl.BlockSpec(memory_space=pl.ANY)
    grad_t, logits_t = pl.pallas_call(
        functools.partial(body, n),
        name="falkon_step",
        out_shape=(
            jax.ShapeDtypeStruct((classes, size), full),
            jax.ShapeDtypeStruct((classes, rows), full),
        ),
        in_specs=[hbm, vmem, hbm, hbm, vmem, vmem],
        out_specs=(vmem, vmem),
        scratch_shapes=[
            pltpu.VMEM((n, size, size), low),
            pltpu.VMEM((chips, rows, features), low),
            pltpu.VMEM((2, size, features), low),
            pltpu.VMEM((chips, 2, rows, size), low),
            pltpu.VMEM((n, classes, size), low),
            pltpu.VMEM((2, classes, size), low),
            pltpu.VMEM((classes, size), full),
            pltpu.VMEM((chips, classes, rows), full),
            pltpu.VMEM((chips, classes, rows), full),
            pltpu.VMEM((chips, classes, rows), low),
            pltpu.VMEM((classes, size), full),
            pltpu.VMEM((classes, size), full),
            pltpu.VMEM((n, classes, size), low),
            pltpu.VMEM((n, classes, size), low),
            pltpu.VMEM((classes, size), full),
            dma((n,)),
            dma((2,)),
            dma((chips,)),
            dma((n,)),
            dma((chips,)),
            dma((3, chips)),
            dma((chips,)),
            dma, dma, dma, dma,
            dma((chips,)),
            dma((chips,)),
            dma((chips,)),
            dma((chips,)),
            dma, dma,
            dma((n,)),
            dma((n,)),
        ],
        compiler_params=pltpu.CompilerParams(
            collective_id=0, has_side_effects=True, vmem_limit_bytes=60 * 1024 * 1024
        ),
    )(points, labels[None, :], centres, tri_inverse, beta.T, bias[:, None])
    return grad_t.T, logits_t.T


def solution(mesh):
    return jax.shard_map(
        on_device,
        mesh=mesh,
        in_specs=(
            P(("groups", "pts"), None),
            P(("groups", "pts")),
            P(("groups", "pts"), None),
            P(("groups", "pts"), None),
            P(("groups", "pts"), None),
            P("groups"),
        ),
        out_specs=(P(("groups", "pts"), None), P(("groups", "pts"), None)),
        check_vma=False,
    )
```

time: 269 us -> 71.3 us (0.27); the launches traced: 266 us -> 71 us
  waiting for transfers between devices: 142 us -> 0 us
  Pallas kernels: 0 us -> 66.2 us
  matrix products: 52.2 us -> 0 us
  blocking collectives: 35.1 us -> 0 us
  local copies, waits for them, and re-layouts: 21.2 us -> 4.13 us
  between operations: 13.8 us -> 0.64 us
    reduce_scatter x2 -> x0, waiting for transfers between devices: 111 us -> none  [the longest x1 57.7 us: on_device(): lax.psum_scatter(term.reshape(lax.axis_size('pts') * dense_centres, 128),...]
    pallas_call x0 -> x1, Pallas kernels: none -> 66.2 us  [on_device(): pl.pallas_call(functools.partial(body, n), name='falkon_step', out_shape=...]
    dot_general x3 -> x0, matrix products: 52.2 us -> none  [the longest x1 23.9 us: on_device(): jnp.dot(kernel_tile, alpha_local, preferred_element_type=jnp.float32)]
    all_gather x2 -> x0, blocking collectives: 35.1 us -> none  [the longest x1 18.7 us: on_device(): beta_part = lax.all_gather(beta_dense, 'pts', axis=0, tiled=True)]
    all_gather x1 -> x0, waiting for transfers between devices: 30.5 us -> none  [on_device(): points_all = lax.all_gather(points, 'pts', axis=0, tiled=True)]
    reshape x7 -> x0, local copies, waits for them, and re-layouts: 13.7 us -> none  [the longest x1 6.46 us: on_device(): term.reshape(lax.axis_size('pts') * dense_centres, 128)]
    dot_general x1 -> x0, local copies, waits for them, and re-layouts: 4.62 us -> none  [on_device(): lax.dot_general(columns, grad_kernel, (((0,), (0,)), ((), ())), preferred...]
  transfers between devices with their start and end apart: 3 -> 0, of which waited for: 3 -> 0; matrix products, arithmetic and copies ran while one was open for 2% -> 0% of each run, Pallas kernels for 0% -> 0%
where the time goes in v2:
time: 71.3 us; the launch traced here: 71 us
  Pallas kernels  66.2 us (93%)
  local copies, waits for them, and re-layouts  4.13 us (6%)
    pallas_call x1, Pallas kernels, on_device(): pl.pallas_call(functools.partial(body, n), name='falkon_step', out_shape=...  66.2 us
    unnamed x2, local copies, waits for them, and re-layouts  2.8 us

profile of v2, /device:TPU:16, one launch (start us, length us, event | category | flops | bytes accessed | tf_op | source)
XLA Modules:
  0.0 71.0 jit_solution(5495943078259407020)
XLA Ops:
  0.6 1.3 %copy.8.bias = f32[16,1]{1,0:T(8,128)} copy(f32[16,1]{0,1:T(1,128)} %bitcast.9) | data formatting | bytes 128 | tf_op jit(solution)/shard_map/broadcast_in_dim | solution.py:377
  2.0 66.2 %falkon_step.1 = (f32[16,1024]{1,0:T(8,128)}, f32[16,256]{1,0:T(8,128)}) custom-call(bf16[256,512]{1,0:T(8,128)(2,1)} %points.1, s32[1,256]{1,0:T(1,128)} %bitcast.8, bf16[1024,512]{1,0:T(8,128)(2,1)} %centres.1, bf16[1024,16384]{1,0:T(8,128)(2,1)} %tri.1, bf16[16,1024]{1,0:T(8,128)(2,1)} %bitcast.6, f32[16,1]{1,0:T(8,128)} %copy.8.bias), custom_call_target="tpu_custom_call" | custom-call | tf_op jit(solution)/shard_map/falkon_step/pallas_call | solution.py:333
  68.2 1.5 %copy.11 = f32[1024,16]{0,1:T(8,128)} copy(f32[1024,16]{0,1:T(8,128)} %bitcast.5) | data formatting | bytes 131072
  69.7 1.3 %copy.12 = f32[256,16]{0,1:T(8,128)} copy(f32[256,16]{0,1:T(8,128)} %bitcast.7) | data formatting | bytes 32768

commit v3 on v2

--- a/solution.py
+++ b/solution.py
@@ -10,6 +10,7 @@
 
 NT = (((1,), (1,)), ((), ()))
 NN = (((1,), (0,)), ((), ()))
+PIECES = 4
 
 
 def dot(left, right, dims):
@@ -83,7 +84,7 @@
 
     @functools.partial(each, chips)
     def _(q):
-        @pl.when(q != chip)
+        @pl.when(q < chip)
         def _():
             beta_send(q).start()
 
@@ -94,30 +95,33 @@
     def chip_of(lev, sid):
         return 2 * lev + sid
 
-    def point_copy(way, block):
+    piece_rows = points.shape[0] // PIECES
+
+    def point_copy(way, block, piece):
         target = (chip + 2, chip - 2, chip_of(level, 1 - side))[way]
+        rows = pbuf.at[block, pl.ds(piece * piece_rows, piece_rows)]
         return remote(
-            pbuf.at[block], pbuf.at[block], p_send.at[way, block], p_recv.at[block],
-            2 * target + core,
+            rows, rows, p_send.at[way, block, piece], p_recv.at[block, piece], 2 * target + core
         )
 
-    def point_sends(lev, act):
+    def point_sends(lev, piece, act):
         block = chip_of(lev, side)
         for way, wanted in (
-            (2, True),
             (0, (lev <= level) & (level < depth - 1)),
             (1, (lev >= level) & (level > 0)),
+            (2, True),
         ):
             @pl.when(wanted)
             def _():
-                act(point_copy(way, block))
+                act(point_copy(way, block, piece))
 
     own_points.wait()
-    point_sends(level, lambda c: c.start())
-
-    @functools.partial(each, chips)
-    def _(q):
-        @pl.when(q != chip)
+    for piece in range(PIECES):
+        point_sends(level, piece, lambda c: c.start())
+
+    @functools.partial(each, chips)
+    def _(q):
+        @pl.when(q > chip)
         def _():
             remote(
                 beta, bbuf.at[2 * q + core], b_send.at[q], b_recv.at[2 * q + core], partner
@@ -138,7 +142,10 @@
     @functools.partial(each, chips)
     def _(q):
         block = 2 * q + 1 - core
-        remote(beta, bbuf.at[block], b_send.at[q], b_recv.at[block], partner).wait_recv()
+
+        @pl.when(q >= chip)
+        def _():
+            remote(beta, bbuf.at[block], b_send.at[q], b_recv.at[block], partner).wait_recv()
 
     asum[...] = jnp.zeros_like(asum)
 
@@ -148,10 +155,12 @@
             tri_copy(j).wait()
             asum[...] += dot(bbuf[j], tbuf[j], NT)
 
+    def piece_wait(block, piece):
+        point_copy(2, block, piece).wait_recv()
+
     def point_wait(block):
-        remote(
-            pbuf.at[block], pbuf.at[block], p_send.at[0, block], p_recv.at[block], partner
-        ).wait_recv()
+        for piece in range(PIECES):
+            piece_wait(block, piece)
 
     share = -(-n // max(depth - 1, 1))
 
@@ -175,15 +184,18 @@
     alpha_pass = remote(abuf.at[core], abuf.at[core], a_send, a_recv, partner)
 
     def step(d):
-        for sign in (-1, 1):
-            lev = level + sign * d
-
-            @pl.when((lev >= 0) & (lev < depth))
-            def _():
-                point_wait(chip_of(lev, side))
-                point_sends(lev, lambda c: c.start())
-
-        each(share, lambda i: add_alpha((d - 1) * share + i))
+        for piece in range(PIECES):
+            for sign in (-1, 1):
+                lev = level + sign * d
+
+                @pl.when((lev >= 0) & (lev < depth))
+                def _():
+                    piece_wait(chip_of(lev, side), piece)
+                    point_sends(lev, piece, lambda c: c.start())
+
+            first = piece * share // PIECES
+            count = (piece + 1) * share // PIECES - first
+            each(count, lambda i: add_alpha((d - 1) * share + first + i))
 
         for sign in (-1, 1):
             lev = level + sign * d
@@ -237,7 +249,11 @@
     logits = lrecv[0]
     for q in range(1, chips):
         logits = logits + lrecv[q]
-    logits = logits + bias[...]
+    spot = lax.broadcasted_iota(jnp.int32, (classes, classes), 0)
+    other = lax.broadcasted_iota(jnp.int32, (classes, classes), 1)
+    row = jnp.broadcast_to(bias[...], (classes, classes))
+    column = jnp.sum(jnp.where(spot == other, row, 0.0), axis=1, keepdims=True)
+    logits = logits + column
     logits_out[...] = logits
     onehot = (labels[...] == lax.broadcasted_iota(jnp.int32, logits.shape, 0)).astype(jnp.float32)
     rbuf[chip] = (jax.nn.sigmoid(logits) - onehot).astype(jnp.bfloat16)
@@ -301,10 +317,16 @@
 
     @functools.partial(each, chips)
     def _(q):
+        @pl.when(q < chip)
+        def _():
+            beta_send(q).wait_send()
+
+        @pl.when(q > chip)
+        def _():
+            beta_pass(q).wait_send()
+
         @pl.when(q != chip)
         def _():
-            beta_send(q).wait_send()
-            beta_pass(q).wait_send()
             logit_copy(q).wait_send()
             resid_copy(q).wait_send()
 
@@ -312,13 +334,19 @@
     centre_pass.wait_send()
     alpha_pass.wait_send()
     grad_pass.wait_send()
-    each(depth, lambda lev: point_sends(lev, lambda c: c.wait_send()))
+    for piece in range(PIECES):
+        each(depth, lambda lev: point_sends(lev, piece, lambda c: c.wait_send()))
 
     @functools.partial(each, n)
     def _(j):
         @pl.when(j > me)
         def _():
             term_copy(j).wait_send()
+
+
+def write_out(grad, logits, grad_out, logits_out):
+    grad_out[...] = grad[...]
+    logits_out[...] = logits[...]
 
 
 def on_device(points, labels, centres, tri_inverse, beta, bias):
@@ -360,8 +388,8 @@
             dma((chips,)),
             dma((n,)),
             dma((chips,)),
-            dma((3, chips)),
-            dma((chips,)),
+            dma((3, chips, PIECES)),
+            dma((chips, PIECES)),
             dma, dma, dma, dma,
             dma((chips,)),
             dma((chips,)),
@@ -374,7 +402,17 @@
         compiler_params=pltpu.CompilerParams(
             collective_id=0, has_side_effects=True, vmem_limit_bytes=60 * 1024 * 1024
         ),
-    )(points, labels[None, :], centres, tri_inverse, beta.T, bias[:, None])
+    )(points, labels[None, :], centres, tri_inverse, beta.T, bias[None, :])
+    grad_t, logits_t = pl.pallas_call(
+        write_out,
+        name="write_out",
+        out_shape=(
+            jax.ShapeDtypeStruct(grad_t.shape, full),
+            jax.ShapeDtypeStruct(logits_t.shape, full),
+        ),
+        in_specs=[vmem, vmem],
+        out_specs=(vmem, vmem),
+    )(grad_t, logits_t)
     return grad_t.T, logits_t.T
 
 

time: 71.3 us -> 66.6 us (0.934)
  local copies, waits for them, and re-layouts: 4.13 us -> 0 us
    unnamed x2 -> x0, local copies, waits for them, and re-layouts: 2.8 us -> none
    pallas_call x1, Pallas kernels: 66.2 us -> 64.2 us  [on_device(): pl.pallas_call(functools.partial(body, n), name='falkon_step', out_shape=...]
    pallas_call x0 -> x1, Pallas kernels: none -> 1.48 us  [on_device(): pl.pallas_call(write_out, name='write_out', out_shape=(jax.ShapeDtypeStru...]
    broadcast_in_dim x1 -> x0, local copies, waits for them, and re-layouts: 1.33 us -> none  [on_device(): bias[:, None]]
where the time goes in v3:
time: 66.6 us; the launch traced here: 66.3 us
  Pallas kernels  65.7 us (99%)
    pallas_call x1, Pallas kernels, on_device(): pl.pallas_call(functools.partial(body, n), name='falkon_step', out_shape=...  64.2 us
    pallas_call x1, Pallas kernels, on_device(): pl.pallas_call(write_out, name='write_out', out_shape=(jax.ShapeDtypeStru...  1.48 us

profile of v3, /device:TPU:16, one launch (start us, length us, event | category | flops | bytes accessed | tf_op | source)
XLA Modules:
  0.0 66.3 jit_solution(12168818812521695699)
XLA Ops:
  0.6 64.2 %falkon_step.1 = (f32[16,1024]{1,0:T(8,128)}, f32[16,256]{1,0:T(8,128)}) custom-call(bf16[256,512]{1,0:T(8,128)(2,1)} %points.1, s32[1,256]{1,0:T(1,128)} %bitcast.6, bf16[1024,512]{1,0:T(8,128)(2,1)} %centres.1, bf16[1024,16384]{1,0:T(8,128)(2,1)} %tri.1, bf16[16,1024]{1,0:T(8,128)(2,1)} %bitcast.5, f32[1,16]{1,0:T(1,128)} %bitcast.7), custom_call_target="tpu_custom_call" | custom-call | tf_op jit(solution)/shard_map/falkon_step/pallas_call | solution.py:361
  64.9 1.5 %write_out.1 = (f32[16,1024]{1,0:T(8,128)}, f32[16,256]{1,0:T(8,128)}) custom-call(f32[16,1024]{1,0:T(8,128)} %get-tuple-element.6.grad, f32[16,256]{1,0:T(8,128)} %get-tuple-element.7.logits), custom_call_target="tpu_custom_call" | custom-call | tf_op jit(solution)/shard_map/write_out/pallas_call | solution.py:406

commit v4 on v3

--- a/solution.py
+++ b/solution.py
@@ -19,9 +19,9 @@
 
 def body(
     n, points, labels, centres, tri, beta, bias, grad_out, logits_out,
-    tbuf, pbuf, cbuf, kbuf, bbuf, abuf, asum, lsend, lrecv, rbuf, gsend, grecv, tsend, trecv, total,
+    tbuf, pbuf, cbuf, kbuf, bbuf, abuf, asum, lsend, lrecv, rbuf, gsend, grecv, tsend, trecv, total, xsend, xrecv, xown,
     t_sem, own_sem, b_send, b_recv, f_send, p_send, p_recv, c_send, c_recv, a_send, a_recv,
-    l_send, l_recv, r_send, r_recv, g_send, g_recv, ts_sem, tr_sem,
+    l_send, l_recv, r_send, r_recv, g_send, g_recv, ts_sem, tr_sem, xs_sem, xr_sem,
 ):
     chips = n // 2
     depth = chips // 2
@@ -286,29 +286,47 @@
     grad_pass.wait_recv()
     coeff = ((mine + grecv[...]) * (1.0 / math.sqrt(total_points))).astype(jnp.bfloat16)
 
-    def term_copy(j):
-        return remote(tsend.at[j], trecv.at[me], ts_sem.at[j], tr_sem.at[me], j)
-
-    @functools.partial(each, n)
+    def term_copy(q):
+        return remote(tsend.at[q], trecv.at[chip], ts_sem.at[q], tr_sem.at[chip], 2 * q + core)
+
+    def pair_copy(q):
+        return remote(xsend.at[q], xrecv.at[q], xs_sem.at[q], xr_sem.at[q], partner)
+
+    def to_pair(q):
+        return (q > chip) | ((q == chip) & (core == 0))
+
+    def finish(q):
+        pair_copy(q).wait_recv()
+        tsend[q] = (xown[q] + xrecv[q]).astype(tsend.dtype)
+        term_copy(q).start()
+
+    @functools.partial(each, chips)
     def _(i):
-        j = n - 1 - i
-
-        @pl.when(j >= me)
-        def _():
-            term = dot(coeff, tbuf[j], NN)
-
-            @pl.when(j == me)
-            def _():
-                total[...] = term
-
-            @pl.when(j != me)
-            def _():
-                tsend[j] = term.astype(tsend.dtype)
-                term_copy(j).start()
-
-    @functools.partial(each, n)
-    def _(q):
-        @pl.when(q < me)
+        q = chips - 1 - i
+
+        @pl.when(to_pair(q))
+        def _():
+            xsend[q] = dot(coeff, tbuf[2 * q + 1 - core], NN)
+            pair_copy(q).start()
+
+        @pl.when(q >= chip)
+        def _():
+            xown[q] = dot(coeff, tbuf[2 * q + core], NN)
+
+        @pl.when((q >= chip) & (q + 1 < chips))
+        def _():
+            finish(q + 1)
+
+    total[...] = xown[chip]
+
+    @pl.when(core == 1)
+    def _():
+        pair_copy(chip).wait_recv()
+        total[...] += xrecv[chip]
+
+    @functools.partial(each, chips)
+    def _(q):
+        @pl.when(q < chip)
         def _():
             remote(tsend.at[q], trecv.at[q], ts_sem.at[q], tr_sem.at[q], partner).wait_recv()
             total[...] += trecv[q].astype(jnp.float32)
@@ -337,11 +355,15 @@
     for piece in range(PIECES):
         each(depth, lambda lev: point_sends(lev, piece, lambda c: c.wait_send()))
 
-    @functools.partial(each, n)
-    def _(j):
-        @pl.when(j > me)
-        def _():
-            term_copy(j).wait_send()
+    @functools.partial(each, chips)
+    def _(q):
+        @pl.when(to_pair(q))
+        def _():
+            pair_copy(q).wait_send()
+
+        @pl.when(q > chip)
+        def _():
+            term_copy(q).wait_send()
 
 
 def write_out(grad, logits, grad_out, logits_out):
@@ -380,9 +402,12 @@
             pltpu.VMEM((chips, classes, rows), low),
             pltpu.VMEM((classes, size), full),
             pltpu.VMEM((classes, size), full),
-            pltpu.VMEM((n, classes, size), low),
-            pltpu.VMEM((n, classes, size), low),
+            pltpu.VMEM((chips, classes, size), low),
+            pltpu.VMEM((chips, classes, size), low),
             pltpu.VMEM((classes, size), full),
+            pltpu.VMEM((chips, classes, size), full),
+            pltpu.VMEM((chips, classes, size), full),
+            pltpu.VMEM((chips, classes, size), full),
             dma((n,)),
             dma((2,)),
             dma((chips,)),
@@ -396,8 +421,10 @@
             dma((chips,)),
             dma((chips,)),
             dma, dma,
-            dma((n,)),
-            dma((n,)),
+            dma((chips,)),
+            dma((chips,)),
+            dma((chips,)),
+            dma((chips,)),
         ],
         compiler_params=pltpu.CompilerParams(
             collective_id=0, has_side_effects=True, vmem_limit_bytes=60 * 1024 * 1024

time: 66.6 us -> 63.4 us (0.952); the launches traced: 66.3 us -> 62.3 us
  Pallas kernels: 65.7 us -> 61.6 us
    pallas_call x1, Pallas kernels: 64.2 us -> 60.1 us  [on_device(): pl.pallas_call(functools.partial(body, n), name='falkon_step', out_shape=...]
where the time goes in v4:
time: 63.4 us; the launch traced here: 62.3 us
  Pallas kernels  61.6 us (97%)
  between operations  0.64 us (1%)
    pallas_call x1, Pallas kernels, on_device(): pl.pallas_call(functools.partial(body, n), name='falkon_step', out_shape=...  60.1 us
    pallas_call x1, Pallas kernels, on_device(): pl.pallas_call(write_out, name='write_out', out_shape=(jax.ShapeDtypeStru...  1.48 us

profile of v4, /device:TPU:16, one launch (start us, length us, event | category | flops | bytes accessed | tf_op | source)
XLA Modules:
  0.0 62.3 jit_solution(13603961853960676798)
XLA Ops:
  0.6 60.1 %falkon_step.1 = (f32[16,1024]{1,0:T(8,128)}, f32[16,256]{1,0:T(8,128)}) custom-call(bf16[256,512]{1,0:T(8,128)(2,1)} %points.1, s32[1,256]{1,0:T(1,128)} %bitcast.6, bf16[1024,512]{1,0:T(8,128)(2,1)} %centres.1, bf16[1024,16384]{1,0:T(8,128)(2,1)} %tri.1, bf16[16,1024]{1,0:T(8,128)(2,1)} %bitcast.5, f32[1,16]{1,0:T(1,128)} %bitcast.7), custom_call_target="tpu_custom_call" | custom-call | tf_op jit(solution)/shard_map/falkon_step/pallas_call | solution.py:383
  60.8 1.5 %write_out.1 = (f32[16,1024]{1,0:T(8,128)}, f32[16,256]{1,0:T(8,128)}) custom-call(f32[16,1024]{1,0:T(8,128)} %get-tuple-element.6.grad, f32[16,256]{1,0:T(8,128)} %get-tuple-element.7.logits), custom_call_target="tpu_custom_call" | custom-call | tf_op jit(solution)/shard_map/write_out/pallas_call | solution.py:433
